TPU v7x, 32 devices: a whole 2x2x4 slice. The times are simulated.
32 devices in a mesh: group: 4 (over x, core), fsdp: 8 (over z, y).
Axes of the slice: x: 2, y: 2, z: 4, core: 2. Of those that a mesh axis runs over, the one named last changes fastest.
Arguments:
- resid_in: bfloat16 [64, 320, 1536], P(('group', 'fsdp')), may hold values from -44 to 44
- attn_out: bfloat16 [64, 320, 1536], P(('group', 'fsdp')), may hold values from -6 to 6
- target_rows: bfloat16 [64, 320, 1536], P(('group', 'fsdp')), may hold values from -6 to 6
- out_weight: bfloat16 [1536, 1536], P('fsdp'), may hold values from -0.15625 to 0.15625
- norm_gain: bfloat16 [1536], replicated, may hold values from 0.099609375 to 1.8984375
- seq_lengths: int32 [64], replicated, may hold values from 33 to 320, as said below
- prompt_ids: int32 [64], replicated, may hold values from 0 to 31, as said below
- log_offsets: float32 [64], replicated, may hold values from -48 to 57
- plan_dest: int32 [64, 5], replicated, may hold values from -1 to 3, as said below
- plan_slot: int32 [64, 5], replicated, may hold values from -1 to 5, as said below
Outputs:
- resid_grad: bfloat16 [64, 320, 1536], P(('group', 'fsdp'))
- attn_grad: bfloat16 [64, 320, 1536], P(('group', 'fsdp'))
- weight_grad: float32 [1536, 1536], P('fsdp')
- loss: float32 [], replicated
Inputs may be any that keep to these rules, and one draw needn't show every extreme that they name: `seq_lengths`: A sequence of length l covers its first ceil(l / 64) buckets; the sequences of one index of fsdp cover exactly 24 buckets together, and on every index of fsdp some device has all 2 sequences of length 320. `plan_dest`: -1 exactly for buckets that the sequence doesn't cover. Among the devices of one index of fsdp, each works on exactly 6 buckets, and no device sends more than 3 of its buckets to one device; some device sends exactly 3 to one device. `plan_slot`: -1 where plan_dest is -1. For one index of fsdp, every pair of working device and position below 6 is taken by exactly one bucket. `prompt_ids`: the sequences of index g along group (g * 2 * 8 onwards) belong to prompts g * 8 to g * 8 + 7, each prompt with exactly 2 sequences.
All inputs are finite; a program needn't handle non-finite values.
Results may differ from a plain program's by a relative error of at most 0.005.
Values may be sent and summed in bfloat16 or wider, within the bound.
No kernel may reach another device: no remote copies, remote signals or barrier semaphores. Data moves between devices by JAX's collectives and lax.ppermute only.
A program may use at most 128 MiB of HBM per device.

v0:
```python
import math

import jax
import jax.numpy as jnp
from jax import lax
from jax.sharding import PartitionSpec as P

PPG = 8


EPS = 1e-06


def forward_rows(x_rows, o_rows, e_rows, weight, gain, mask):
    width = x_rows.shape[-1]
    mixed = x_rows.astype(jnp.float32) + jnp.dot(o_rows, weight, preferred_element_type=jnp.float32)
    scale_inv = lax.rsqrt(jnp.mean(mixed * mixed, axis=-1, keepdims=True) + EPS)
    normed = mixed * scale_inv * gain.astype(jnp.float32)
    token_logp = jnp.sum(normed * e_rows.astype(jnp.float32), axis=-1) * mask / math.sqrt(width)
    return (mixed, scale_inv, token_logp)


def backward_rows(mixed, scale_inv, e_rows, gain, coeff, weight):
    width = mixed.shape[-1]
    gained = (
        coeff[:, None] * e_rows.astype(jnp.float32) * gain.astype(jnp.float32) / math.sqrt(width)
    )
    inner = jnp.mean(mixed * gained, axis=-1, keepdims=True)
    grad_rows = (scale_inv * gained - mixed * scale_inv**3 * inner).astype(jnp.bfloat16)
    attn_rows = lax.dot_general(
        grad_rows, weight, (((1,), (1,)), ((), ())), preferred_element_type=jnp.float32
    ).astype(jnp.bfloat16)
    return (grad_rows, attn_rows)


def local(
    resid_in,
    attn_out,
    target_rows,
    out_weight,
    norm_gain,
    seq_lengths,
    prompt_ids,
    log_offsets,
    plan_dest,
    plan_slot,
):
    seq_dev, lmax, width = resid_in.shape
    n_group = lax.axis_size("group")
    n_fsdp = lax.axis_size("fsdp")
    group_idx = lax.axis_index("group")
    fsdp_idx = lax.axis_index("fsdp")
    total_seqs = seq_lengths.shape[0]
    prompts = PPG * n_group
    samples = seq_dev * n_fsdp // PPG
    prompt_range = jnp.arange(prompts, dtype=jnp.int32)
    weight = lax.all_gather(out_weight, "fsdp", axis=0, tiled=True)
    first = (group_idx * n_fsdp + fsdp_idx) * seq_dev
    my_len = lax.dynamic_slice_in_dim(seq_lengths, first, seq_dev)
    positions = jnp.arange(lmax, dtype=jnp.int32)
    mask = (positions[None, :] < my_len[:, None]).astype(jnp.float32).reshape(-1)
    x_rows = resid_in.reshape(-1, width)
    o_rows = attn_out.reshape(-1, width)
    e_rows = target_rows.reshape(-1, width)
    mixed, scale_inv, token_logp = forward_rows(x_rows, o_rows, e_rows, weight, norm_gain, mask)
    seq_logp = jnp.sum(token_logp.reshape(seq_dev, lmax), axis=1)
    delta = seq_logp + lax.dynamic_slice_in_dim(log_offsets, first, seq_dev)
    my_prompt = lax.dynamic_slice_in_dim(prompt_ids, first, seq_dev)
    member = (my_prompt[:, None] == prompt_range[None, :]).astype(jnp.float32)
    prompt_part = jnp.sum(member * delta[:, None], axis=0)
    prompt_total = lax.psum(prompt_part, "fsdp")
    baseline = prompt_total / samples
    centred = delta - jnp.sum(member * baseline[None, :], axis=1)
    square_total = lax.psum(jnp.sum(centred * centred), ("group", "fsdp"))
    coeff = jnp.repeat(centred, lmax) * mask
    grad_rows, attn_rows = backward_rows(mixed, scale_inv, e_rows, norm_gain, coeff, weight)
    resid_grad = grad_rows.reshape(seq_dev, lmax, width)
    attn_grad = attn_rows.reshape(seq_dev, lmax, width)
    part_rows = lax.psum_scatter(
        lax.dot_general(
            o_rows, grad_rows, (((0,), (0,)), ((), ())), preferred_element_type=jnp.float32
        ),
        "fsdp",
        scatter_dimension=0,
        tiled=True,
    )
    weight_grad = lax.psum(part_rows, "group") / total_seqs
    loss = square_total / (total_seqs * lmax)
    return (resid_grad, attn_grad, weight_grad, loss)


def solution(mesh):
    return jax.shard_map(
        local,
        mesh=mesh,
        in_specs=(
            P(("group", "fsdp"), None, None),
            P(("group", "fsdp"), None, None),
            P(("group", "fsdp"), None, None),
            P("fsdp", None),
            P(),
            P(),
            P(),
            P(),
            P(),
            P(),
        ),
        out_specs=(
            P(("group", "fsdp"), None, None),
            P(("group", "fsdp"), None, None),
            P("fsdp", None),
            P(),
        ),
        check_vma=False,
    )
```

profile of v0, /device:TPU:0, one launch (start us, length us, event | category | flops | bytes accessed | tf_op | source)
XLA Modules:
  0.0 360.7 jit_solution(16981682612720377899)
XLA Ops:
  7.2 0.0 copy-start
  7.2 0.0 all-gather.2.cloned.1.call-start
  7.2 0.7 all-gather.2.cloned.1.call-update
  7.9 0.0 reduce-scatter.4.cloned.1.call-start
  8.0 0.7 dynamic_slice.9
  8.7 0.7 dynamic_slice.11
  9.4 0.7 convert_element_type.30
  10.1 82.1 %all-gather.2.cloned.1.call-done = bf16[1536,1536]{1,0:T(8,128)(2,1)} async-done(((bf16[192,1536]{1,0:T(8,128)(2,1)}), bf16[1536,1536]{1,0:T(8,128)(2,1)}) %all-gather.2.cloned.1.call-update) | async-done | bytes 4718608 | tf_op jit(solution)/shard_map/all_gather | solution.py:57
  92.3 0.0 copy-done
  92.3 0.0 copy-start.3
  92.3 6.4 %multiply_reduce_fusion = (f32[640]{0:T(1024)S(1)}, f32[640,1536]{1,0:T(8,128)S(1)}) fusion(bf16[640,1536]{1,0:T(8,128)(2,1)S(1)} %bitcast.19, bf16[1536,1536]{1,0:T(8,128)(2,1)} %all-gather.2.cloned.1.call-done, bf16[640,1536]{1,0:T(8,128)(2,1)} %bitcast.22), kind=kOutput, calls=%fused_computation.12 | convolution fusion | flops 3023830528 | bytes 12585472 | tf_op jit(solution)/shard_map/dot_general | solution.py:16
  98.7 0.0 copy-start.1
  98.7 0.0 copy-start.6
  98.7 1.8 copy-done.1
  100.6 0.0 copy-done.3
  100.6 0.8 fusion
  101.3 0.1 reduce_sum.67
  101.4 0.2 multiply_reduce_fusion.1
  101.6 0.0 copy-done.6
  101.6 0.1 dynamic-slice_add_fusion
  101.7 0.1 select_reduce_fusion.1
  101.8 18.8 %psum.21 = f32[32]{0:T(128)S(1)} all-reduce(f32[32]{0:T(128)S(1)} %select_reduce_fusion.1), channel_id=1, replica_groups=mesh['group'=4,'fsdp'=8] {'fsdp'}, use_global_device_ids=true, to_apply=%region_4.0 | all-reduce | flops 32 | bytes 256 | tf_op jit(solution)/shard_map/psum | solution.py:71
  120.6 0.2 select_reduce_fusion
  120.8 0.6 multiply_reduce_fusion.2
  121.4 0.1 fusion.8
  121.4 0.1 mul.116
  121.5 0.0 copy-start.2
  121.5 0.0 copy-start.4
  121.5 3.8 %fusion.7 = f32[640]{0:T(1024)S(1)} fusion(f32[640,1536]{1,0:T(8,128)} %copy-done.1, bf16[2,320,1536]{2,1,0:T(8,128)(2,1)} %param.12, f32[640]{0:T(1024)S(1)} %mul.116, f32[1536]{0:T(1024)S(1)} %convert_element_type.30), kind=kLoop, calls=%fused_computation.10 | loop fusion | flops 5897600 | bytes 5909504 | tf_op jit(solution)/shard_map/reduce_sum | solution.py:28
  125.3 0.1 copy-done.2
  125.4 0.6 copy-done.4
  126.0 1.2 fusion.5
  127.2 0.0 copy-start.5
  127.2 1.3 copy-done.5
  128.5 6.3 %convolution_bitcast_fusion = f32[1536,1536]{0,1:T(8,128)} fusion(bf16[640,1536]{1,0:T(8,128)(2,1)S(1)} %fusion.5, bf16[640,1536]{1,0:T(8,128)(2,1)S(1)} %bitcast.20), kind=kOutput, calls=%fused_computation | convolution fusion | flops 3019898880 | bytes 13369344 | tf_op jit(solution)/shard_map/dot_general | solution.py:80
  134.8 9.6 %copy.15 = f32[1536,1536]{1,0:T(8,128)} copy(f32[1536,1536]{0,1:T(8,128)} %convolution_bitcast_fusion) | data formatting | bytes 18874368
  144.4 0.0 reduce-scatter.4.cloned.1.call-update
  144.5 0.0 all-reduce.2.cloned.1.call-start
  144.5 41.5 %psum.23 = f32[]{:T(128)} all-reduce(f32[]{:T(128)} %get-tuple-element.16), channel_id=1, replica_groups=mesh['group'=4,'fsdp'=8] {'group','fsdp'}, use_global_device_ids=true, to_apply=%region_10.0 | all-reduce | flops 1 | bytes 8 | tf_op jit(solution)/shard_map/psum | solution.py:74
  186.6 118.4 %reduce-scatter.4.cloned.1.call-done = f32[192,1536]{1,0:T(8,128)} async-done(((f32[1536,1536]{1,0:T(8,128)}), f32[192,1536]{1,0:T(8,128)}) %reduce-scatter.4.cloned.1.call-update) | async-done | bytes 1179664
  305.0 2.9 copy.16
  307.9 0.0 all-reduce.2.cloned.1.call-update
  308.0 7.4 %convolution_convert_fusion = bf16[640,1536]{1,0:T(8,128)(2,1)} fusion(bf16[640,1536]{1,0:T(8,128)(2,1)} %copy-done.5, bf16[1536,1536]{1,0:T(8,128)(2,1)} %all-gather.2.cloned.1.call-done), kind=kOutput, calls=%fused_computation.13 | convolution fusion | flops 3020881920 | bytes 8650752 | tf_op jit(solution)/shard_map/dot_general | solution.py:30
  315.4 34.6 %all-reduce.2.cloned.1.call-done = f32[192,1536]{0,1:T(8,128)} async-done(((f32[192,1536]{0,1:T(8,128)}), f32[192,1536]{0,1:T(8,128)}) %all-reduce.2.cloned.1.call-update) | async-done | bytes 1179664 | tf_op jit(solution)/shard_map/psum | solution.py:87
  350.1 1.5 broadcast_multiply_fusion
  351.6 1.5 copy.14
  (3 shorter events, 0.0 us)
Async XLA Ops:
  7.2 85.1 %copy-start = (bf16[2,320,1536]{2,1,0:T(8,128)(2,1)S(1)}, bf16[2,320,1536]{2,1,0:T(8,128)(2,1)}, u32[]{:S(2)}) copy-start(bf16[2,320,1536]{2,1,0:T(8,128)(2,1)} %param.11) | copy-start | bytes 5898244
  7.2 85.1 %all-gather.2.cloned.1.call-start = ((), (), s32[]{:S(2)}) async-start(), calls=%async_computation.1 | async-start | bytes 5308416 | tf_op jit(solution)/shard_map/all_gather | solution.py:57
  7.9 297.1 %reduce-scatter.4.cloned.1.call-start = ((), (), s32[]{:S(2)}) async-start(), calls=%async_computation.3 | async-start | bytes 10616832
  92.3 8.3 %copy-start.3 = (bf16[2,320,1536]{2,1,0:T(8,128)(2,1)S(1)}, bf16[2,320,1536]{2,1,0:T(8,128)(2,1)}, u32[]{:S(2)}) copy-start(bf16[2,320,1536]{2,1,0:T(8,128)(2,1)} %param.12) | copy-start | bytes 5898244
  98.7 1.9 copy-start.1
  98.7 2.9 copy-start.6
  121.5 3.9 %copy-start.2 = (f32[640,1536]{1,0:T(8,128)S(1)}, f32[640,1536]{1,0:T(8,128)}, u32[]{:S(2)}) copy-start(f32[640,1536]{1,0:T(8,128)} %copy-done.1) | copy-start | bytes 11796484
  121.5 4.5 %copy-start.4 = (bf16[2,320,1536]{2,1,0:T(8,128)(2,1)S(1)}, bf16[2,320,1536]{2,1,0:T(8,128)(2,1)}, u32[]{:S(2)}) copy-start(bf16[2,320,1536]{2,1,0:T(8,128)(2,1)} %param.12) | copy-start | bytes 5898244
  127.2 1.3 copy-start.5
  144.5 205.6 %all-reduce.2.cloned.1.call-start = ((), (), s32[]{:S(2)}) async-start(), calls=%async_computation.2 | async-start | bytes 3145728 | tf_op jit(solution)/shard_map/psum | solution.py:87
Sparse Core Ops, SparseCore 0:
  10.2 82.0 all-gather.1
  144.6 160.4 reduce-scatter.3
  308.1 41.9 all-reduce.1
where the time goes:
time: 361 us
  waiting for transfers between devices  236 us (65%)
  blocking collectives  60.2 us (17%)
  matrix products  20.2 us (6%)
  local copies, waits for them, and re-layouts  19.4 us (5%)
  between operations  15.6 us (4%)
  other arithmetic  9.2 us (3%)
    unnamed x4, waiting for transfers between devices  119 us
    all_gather x1, waiting for transfers between devices, local(): weight = lax.all_gather(out_weight, 'fsdp', axis=0, tiled=True)  82.1 us
    psum x1, blocking collectives, local(): square_total = lax.psum(jnp.sum(centred * centred), ('group', 'fsdp'))  41.5 us
    psum x1, waiting for transfers between devices, local(): weight_grad = lax.psum(part_rows, 'group') / total_seqs  34.6 us
    psum x1, blocking collectives, local(): prompt_total = lax.psum(prompt_part, 'fsdp')  18.8 us
    unnamed x17, local copies, waits for them, and re-layouts  17.8 us
    dot_general x1, matrix products, backward_rows(): lax.dot_general(grad_rows, weight, (((1,), (1,)), ((), ())), preferred_el...  7.45 us
  transfers between devices with their start and end apart: 3, of which 3 were waited for; matrix products, arithmetic and copies ran while one was open for 3% of the time, Pallas kernels for 0%

commit v1 on v0

v1 whole, which is shorter than its diff:
```python
import functools
import math

import jax
import jax.numpy as jnp
import numpy as np
from jax import lax
from jax.experimental import pallas as pl
from jax.experimental.pallas import tpu as pltpu
from jax.sharding import PartitionSpec as P

PPG = 8
EPS = 1e-06
BOTH = ("group", "fsdp")


def ring_order(n):
    y = 1
    while 2 * y * y < n:
        y *= 2
    if 2 * y * y != n or y < 2:
        return list(range(n))
    z = n // y
    cells = [(k, 0) for k in range(z)]
    for turn, k in enumerate(reversed(range(z))):
        row = range(1, y) if turn % 2 == 0 else range(y - 1, 0, -1)
        cells += [(k, j) for j in row]
    return [k * y + j for k, j in cells]


def ring_table(n):
    order = ring_order(n)
    pos = {f: p for p, f in enumerate(order)}
    table = np.zeros((2, n, n), np.int32)
    for c in range(2):
        sign = 1 if c == 0 else -1
        for f in range(n):
            for d in range(n):
                table[c, f, d] = order[(pos[f] + sign * d) % n]
    return table


def copy_shards(n, meta, table, shards, wbuf, sems):
    rows = shards[0].shape[0]
    base = (lax.rem(meta[0], 2) * n + meta[1]) * n
    half = n // 2
    steps = [0] + [n - k for k in range(1, half)] + list(range(1, half)) + [half]
    copies = []
    for at, (d, shard) in enumerate(zip(steps, shards)):
        first = pl.multiple_of(table[base + d] * rows, 16)
        copies.append(pltpu.make_async_copy(shard, wbuf.at[pl.ds(first, rows), :], sems.at[at]))
    for copy in copies:
        copy.start()
    for copy in copies:
        copy.wait()


def forward_kernel(n, seq_dev, lmax, bt, meta, table, lens, offs, o_ref, x_ref, e_ref, gain_ref, *rest):
    shards, (r_ref, pay_ref, wbuf, sums, sems) = rest[:n], rest[n:]
    step = pl.program_id(0)
    blocks = lmax // bt
    width = o_ref.shape[-1]

    @pl.when(step == 0)
    def _():
        copy_shards(n, meta, table, shards, wbuf, sems)
        for s in range(seq_dev):
            sums[s] = 0.0

    first = (meta[0] * n + meta[1]) * seq_dev
    seq = step // blocks
    mixed = x_ref[0].astype(jnp.float32) + jnp.dot(
        o_ref[0], wbuf[...], preferred_element_type=jnp.float32
    )
    scale_inv = lax.rsqrt(jnp.mean(mixed * mixed, axis=-1, keepdims=True) + EPS)
    gained = e_ref[0].astype(jnp.float32) * (gain_ref[...].astype(jnp.float32) / math.sqrt(width))
    inner = jnp.sum(mixed * gained, axis=-1, keepdims=True)
    token = lax.rem(step, blocks) * bt + lax.broadcasted_iota(jnp.int32, (bt, 1), 0)
    covered = token < lens[first + seq]
    logp = jnp.where(covered, inner * scale_inv, 0.0)
    sums[seq] += jnp.sum(logp)
    keep = jnp.where(covered, scale_inv, 0.0)
    pull = scale_inv * scale_inv * (inner / width)
    r_ref[0] = (keep * (gained - mixed * pull)).astype(r_ref.dtype)

    @pl.when(step == pl.num_programs(0) - 1)
    def _():
        lane = lax.broadcasted_iota(jnp.int32, pay_ref.shape, 2)
        pay = jnp.zeros(pay_ref.shape, jnp.float32)
        for s in range(seq_dev):
            pay = jnp.where(lane == s, sums[s] + offs[first + s], pay)
        pay_ref[...] = pay


def contract(coeffs, ot_own, ot_par, r_own, r_par, cols):
    total = None
    seq_dev = ot_own.shape[0]
    for q, c in enumerate(coeffs):
        ot, r, s = (ot_own, r_own, q) if q < seq_dev else (ot_par, r_par, q - seq_dev)
        part = c * jnp.dot(ot[s], r[s, :, cols], preferred_element_type=jnp.float32)
        total = part if total is None else total + part
    return total


def first_kernel(n, seq_dev, samples, meta, table, pids, recv, pidm, ot_own, ot_par, r_own, r_par, out, c_ref):
    me = meta[0] * n + meta[1]
    core = lax.rem(meta[0], 2)
    par = me + (1 - 2 * core) * n
    dm = recv[:, 0, :]
    ids = pidm[...]
    row = lax.broadcasted_iota(jnp.int32, dm.shape, 0)
    lane = lax.broadcasted_iota(jnp.int32, dm.shape, 1)
    coeffs = []
    for q in range(2 * seq_dev):
        dev, s = (me, q) if q < seq_dev else (par, q - seq_dev)
        pid = pids[dev * seq_dev + s]
        own = jnp.where((row == dev) & (lane == s), dm, 0.0)
        same = jnp.where(ids == pid, dm, 0.0)
        coeffs.append(jnp.sum(own, keepdims=True) - jnp.sum(same, keepdims=True) / samples)
    for q, c in enumerate(coeffs):
        c_ref[q : q + 1, :] = jnp.broadcast_to(c, (1, c_ref.shape[1]))
    out[...] = contract(coeffs, ot_own, ot_par, r_own, r_par, slice(None)).astype(out.dtype)


def rest_kernel(n, seq_dev, meta, table, c_ref, ot_own, ot_par, r_own, r_par, out):
    step = pl.program_id(0)
    core = lax.rem(meta[0], 2)
    half = jnp.where(lax.rem(step, 2) == 0, core, 1 - core)
    cols = out.shape[-1]
    take = pl.ds(pl.multiple_of(half * cols, 128), cols)
    coeffs = [c_ref[q : q + 1, 0:1] for q in range(2 * seq_dev)]
    out[0] = contract(coeffs, ot_own, ot_par, r_own, r_par, take).astype(out.dtype)


def attn_kernel(n, blocks, meta, table, c_ref, r_ref, *rest):
    shards, (g_ref, a_ref, wbuf, sems) = rest[:n], rest[n:]
    step = pl.program_id(0)

    @pl.when(step == 0)
    def _():
        copy_shards(n, meta, table, shards, wbuf, sems)

    c = c_ref[pl.ds(step // blocks, 1), 0:1]
    r = r_ref[0]
    g_ref[0] = (c * r.astype(jnp.float32)).astype(g_ref.dtype)
    rows = lax.dot_general(
        r, wbuf[...], (((1,), (1,)), ((), ())), preferred_element_type=jnp.float32
    )
    a_ref[0] = (c * rows).astype(a_ref.dtype)


def local(
    order,
    resid_in,
    attn_out,
    target_rows,
    out_weight,
    norm_gain,
    seq_lengths,
    prompt_ids,
    log_offsets,
    plan_dest,
    plan_slot,
):
    seq_dev, lmax, width = resid_in.shape
    rows = out_weight.shape[0]
    n_group = lax.axis_size("group")
    n = lax.axis_size("fsdp")
    n_dev = n_group * n
    half_n = n // 2
    half_w = width // 2
    total_seqs = seq_lengths.shape[0]
    prompts = PPG * n_group
    samples = seq_dev * n // PPG
    group_idx = lax.axis_index("group")
    fsdp_idx = lax.axis_index("fsdp")
    bt = lmax // 2
    blocks = lmax // bt
    bf16, f32 = jnp.bfloat16, jnp.float32
    any_spec = pl.BlockSpec(memory_space=pl.ANY)

    along = []
    for g in range(n_group):
        sign = 1 if g % 2 == 0 else -1
        for p in range(n):
            along.append((g * n + order[p], g * n + order[(p + sign) % n]))
    pair = [(g, g ^ 1) for g in range(n_group)]

    def ring(value):
        return lax.ppermute(value, BOTH, along)

    def swap(value):
        return lax.ppermute(value, "group", pair)

    behind, ahead = [], []
    piece = out_weight
    for _ in range(half_n - 1):
        piece = ring(piece)
        behind.append(piece)
        ahead.append(swap(piece))
    opposite = ring(piece)
    shards = [out_weight, *behind, *ahead, opposite]

    ot_own = jnp.swapaxes(attn_out, 1, 2)
    ot_par = swap(ot_own)

    meta = jnp.stack([group_idx, fsdp_idx]).astype(jnp.int32)
    table = jnp.asarray(ring_table(n).reshape(-1))
    gain = norm_gain.reshape(1, width)
    pidm = jnp.pad(
        prompt_ids.reshape(n_dev, seq_dev), ((0, 0), (0, 128 - seq_dev)), constant_values=-1
    )

    flops = 2 * seq_dev * lmax * width * width
    token_block = pl.BlockSpec((1, bt, width), lambda i, *_: (i // blocks, i % blocks, 0))
    r_own, pay = pl.pallas_call(
        functools.partial(forward_kernel, n, seq_dev, lmax, bt),
        grid_spec=pltpu.PrefetchScalarGridSpec(
            num_scalar_prefetch=4,
            grid=(seq_dev * blocks,),
            in_specs=[token_block] * 3
            + [pl.BlockSpec((1, width), lambda i, *_: (0, 0))]
            + [any_spec] * n,
            out_specs=[
                token_block,
                pl.BlockSpec((n_dev, 8, 128), lambda i, *_: (0, 0, 0)),
            ],
            scratch_shapes=[
                pltpu.VMEM((width, width), bf16),
                pltpu.SMEM((seq_dev,), f32),
                pltpu.SemaphoreType.DMA((n,)),
            ],
        ),
        out_shape=[
            jax.ShapeDtypeStruct((seq_dev, lmax, width), bf16),
            jax.ShapeDtypeStruct((n_dev, 8, 128), f32),
        ],
        cost_estimate=pl.CostEstimate(
            flops=flops, bytes_accessed=2 * width * (width + 4 * seq_dev * lmax), transcendentals=0
        ),
        name="forward_rows",
    )(meta, table, seq_lengths, log_offsets, attn_out, resid_in, target_rows, gain, *shards)

    r_par = swap(r_own)
    recv = lax.all_to_all(pay, BOTH, 0, 0, tiled=True)

    def row_block(d):
        def index(i, meta, table, *_):
            return (0, table[((meta[0] % 2) * n + meta[1]) * n + d], 0)

        return index

    def rest_rows(i, meta, table, *_):
        return (0, table[((meta[0] % 2) * n + meta[1]) * n + half_n - 1 - i // 2], 0)

    sent, coeff = pl.pallas_call(
        functools.partial(first_kernel, n, seq_dev, samples),
        grid_spec=pltpu.PrefetchScalarGridSpec(
            num_scalar_prefetch=3,
            grid=(1,),
            in_specs=[
                pl.BlockSpec((n_dev, 8, 128), lambda i, *_: (0, 0, 0)),
                pl.BlockSpec((n_dev, 128), lambda i, *_: (0, 0)),
                pl.BlockSpec((seq_dev, rows, lmax), row_block(half_n)),
                pl.BlockSpec((seq_dev, rows, lmax), row_block(half_n)),
                pl.BlockSpec((seq_dev, lmax, half_w), lambda i, meta, *_: (0, 0, meta[0] % 2)),
                pl.BlockSpec((seq_dev, lmax, half_w), lambda i, meta, *_: (0, 0, meta[0] % 2)),
            ],
            out_specs=[
                pl.BlockSpec((rows, half_w), lambda i, *_: (0, 0)),
                pl.BlockSpec((8, 128), lambda i, *_: (0, 0)),
            ],
        ),
        out_shape=[
            jax.ShapeDtypeStruct((rows, half_w), bf16),
            jax.ShapeDtypeStruct((8, 128), f32),
        ],
        cost_estimate=pl.CostEstimate(
            flops=2 * flops // n // 2,
            bytes_accessed=2 * 2 * seq_dev * lmax * (half_w + rows),
            transcendentals=0,
        ),
        name="first_rows",
    )(meta, table, prompt_ids, recv, pidm, ot_own, ot_par, r_own, r_par)

    got = ring(sent)

    parts = pl.pallas_call(
        functools.partial(rest_kernel, n, seq_dev),
        grid_spec=pltpu.PrefetchScalarGridSpec(
            num_scalar_prefetch=2,
            grid=(n - 1,),
            in_specs=[
                pl.BlockSpec((8, 128), lambda i, *_: (0, 0)),
                pl.BlockSpec((seq_dev, rows, lmax), rest_rows),
                pl.BlockSpec((seq_dev, rows, lmax), rest_rows),
                pl.BlockSpec((seq_dev, lmax, width), lambda i, *_: (0, 0, 0)),
                pl.BlockSpec((seq_dev, lmax, width), lambda i, *_: (0, 0, 0)),
            ],
            out_specs=pl.BlockSpec((1, rows, half_w), lambda i, *_: (i, 0, 0)),
        ),
        out_shape=jax.ShapeDtypeStruct((n - 1, rows, half_w), bf16),
        cost_estimate=pl.CostEstimate(
            flops=flops,
            bytes_accessed=2 * 4 * seq_dev * lmax * width + width * width,
            transcendentals=0,
        ),
        name="rest_rows",
    )(meta, table, coeff, ot_own, ot_par, r_own, r_par)

    resid_grad, attn_grad = pl.pallas_call(
        functools.partial(attn_kernel, n, blocks),
        grid_spec=pltpu.PrefetchScalarGridSpec(
            num_scalar_prefetch=2,
            grid=(seq_dev * blocks,),
            in_specs=[pl.BlockSpec((8, 128), lambda i, *_: (0, 0)), token_block] + [any_spec] * n,
            out_specs=[token_block, token_block],
            scratch_shapes=[
                pltpu.VMEM((width, width), bf16),
                pltpu.SemaphoreType.DMA((n,)),
            ],
        ),
        out_shape=[jax.ShapeDtypeStruct((seq_dev, lmax, width), bf16)] * 2,
        cost_estimate=pl.CostEstimate(
            flops=flops, bytes_accessed=2 * width * (width + 3 * seq_dev * lmax), transcendentals=0
        ),
        name="attn_rows",
    )(meta, table, coeff, r_own, *shards)

    def add(a, b):
        return (a.astype(f32) + b.astype(f32)).astype(bf16)

    run = jnp.stack([add(got, parts[0]), parts[1]])
    for k in range(1, half_n):
        run = ring(run)
        if k < half_n - 1:
            run = add(run, parts[2 * k : 2 * k + 2])
    run = run.astype(f32)
    mine = (run[0] + parts[n - 2].astype(f32) + swap(run[1].astype(bf16)).astype(f32)).astype(bf16)
    bit = 2
    while bit < n_group:
        other = lax.ppermute(mine, "group", [(g, g ^ bit) for g in range(n_group)])
        whole = mine.astype(f32) + other.astype(f32)
        mine = whole.astype(bf16)
        bit *= 2
    whole = whole / total_seqs
    other = swap(whole)
    low = lax.rem(group_idx, 2) == 0
    weight_grad = jnp.concatenate(
        [jnp.where(low, whole, other), jnp.where(low, other, whole)], axis=1
    )

    delta = recv[:, 0, :seq_dev].reshape(-1)
    member = (prompt_ids[:, None] == jnp.arange(prompts, dtype=jnp.int32)[None, :]).astype(f32)
    baseline = jnp.sum(member * delta[:, None], axis=0) / samples
    centred = delta - jnp.sum(member * baseline[None, :], axis=1)
    loss = jnp.sum(centred * centred) / (total_seqs * lmax)
    return (resid_grad, attn_grad, weight_grad, loss)


def solution(mesh):
    order = ring_order(mesh.shape["fsdp"])
    return jax.shard_map(
        functools.partial(local, order),
        mesh=mesh,
        in_specs=(
            P(("group", "fsdp"), None, None),
            P(("group", "fsdp"), None, None),
            P(("group", "fsdp"), None, None),
            P("fsdp", None),
            P(),
            P(),
            P(),
            P(),
            P(),
            P(),
        ),
        out_specs=(
            P(("group", "fsdp"), None, None),
            P(("group", "fsdp"), None, None),
            P("fsdp", None),
            P(),
        ),
        check_vma=False,
    )
```

time: 361 us -> 145 us (0.40)
  waiting for transfers between devices: 236 us -> 62.6 us
  blocking collectives: 60.2 us -> 0 us
  Pallas kernels: 0 us -> 37.7 us
  starting transfers between devices: 0.12 us -> 24.4 us
  matrix products: 20.2 us -> 0 us
  between operations: 15.6 us -> 2.61 us
  local copies, waits for them, and re-layouts: 19.4 us -> 11.5 us
  other arithmetic: 9.2 us -> 5.26 us
    unnamed x4 -> x0, waiting for transfers between devices: 119 us -> none
    all_gather x1 -> x0, waiting for transfers between devices: 82.1 us -> none  [local(): weight = lax.all_gather(out_weight, 'fsdp', axis=0, tiled=True)]
    ppermute x0 -> x16, waiting for transfers between devices: none -> 62.1 us  [the longest x8 54.1 us: ring(): return lax.ppermute(value, BOTH, along)]
    psum x2 -> x0, blocking collectives: 60.2 us -> none  [the longest x1 41.5 us: local(): square_total = lax.psum(jnp.sum(centred * centred), ('group', 'fsdp'))]
    pallas_call x0 -> x4, Pallas kernels: none -> 37.7 us  [the longest x1 12.2 us: local(): pl.pallas_call(functools.partial(attn_kernel, n, blocks), grid_spec=pltpu...]
    psum x1 -> x0, waiting for transfers between devices: 34.6 us -> none  [local(): weight_grad = lax.psum(part_rows, 'group') / total_seqs]
    dot_general x3 -> x0, matrix products: 20.2 us -> none  [the longest x1 7.45 us: backward_rows(): lax.dot_general(grad_rows, weight, (((1,), (1,)), ((), ())), preferred_el...]
    ppermute x0 -> x16, starting transfers between devices: none -> 18 us  [the longest x8 15.2 us: ring(): return lax.ppermute(value, BOTH, along)]
  transfers between devices with their start and end apart: 3 -> 17, of which waited for: 3 -> 10; matrix products, arithmetic and copies ran while one was open for 3% -> 9% of each run, Pallas kernels for 0% -> 23%
where the time goes in v1:
time: 145 us; the launch traced here: 144 us
  waiting for transfers between devices  62.6 us (43%)
  Pallas kernels  37.7 us (26%)
  starting transfers between devices  24.4 us (17%)
  local copies, waits for them, and re-layouts  11.5 us (8%)
  other arithmetic  5.26 us (4%)
  between operations  2.61 us (2%)
    ppermute x8, waiting for transfers between devices, ring(): return lax.ppermute(value, BOTH, along)  54.1 us
    ppermute x8, starting transfers between devices, ring(): return lax.ppermute(value, BOTH, along)  15.2 us
    pallas_call x1, Pallas kernels, local(): pl.pallas_call(functools.partial(attn_kernel, n, blocks), grid_spec=pltpu...  12.2 us
    pallas_call x1, Pallas kernels, local(): pl.pallas_call(functools.partial(forward_kernel, n, seq_dev, lmax, bt), g...  11 us
    pallas_call x1, Pallas kernels, local(): pl.pallas_call(functools.partial(rest_kernel, n, seq_dev), grid_spec=pltp...  10.6 us
    all_to_all x1, starting transfers between devices, local(): recv = lax.all_to_all(pay, BOTH, 0, 0, tiled=True)  6.45 us
    ppermute x1, waiting for transfers between devices, local(): other = lax.ppermute(mine, 'group', [(g, g ^ bit) for g in range(n_group)])  6.41 us
    ppermute x1, local copies, waits for them, and re-layouts, swap(): return lax.ppermute(value, 'group', pair)  4.09 us
  transfers between devices with their start and end apart: 17, of which 10 were waited for; matrix products, arithmetic and copies ran while one was open for 9% of the time, Pallas kernels for 23%

profile of v1, /device:TPU:0, one launch (start us, length us, event | category | flops | bytes accessed | tf_op | source)
XLA Modules:
  0.0 144.0 jit_solution(4472252327163305833)
XLA Ops:
  0.6 3.1 %collective-permute-start = (bf16[192,1536]{1,0:T(8,128)(2,1)}, bf16[192,1536]{1,0:T(8,128)(2,1)S(1)}, u32[]{:S(2)}, u32[]{:S(2)}) collective-permute-start(bf16[192,1536]{1,0:T(8,128)(2,1)} %rest_0_.3), channel_id=1, source_target_pairs={{0,2},{2,4},{4,6},{6,7},{7,5},{5,3},{3,1},{1,0},{8,9},{10,8},{12,1... | collective-permute-start | bytes 1769480 | tf_op jit(solution)/shard_map/ppermute | solution.py:190
  3.7 8.0 %collective-permute-done.rest_1_ = bf16[192,1536]{1,0:T(8,128)(2,1)S(1)} collective-permute-done((bf16[192,1536]{1,0:T(8,128)(2,1)}, bf16[192,1536]{1,0:T(8,128)(2,1)S(1)}, u32[]{:S(2)}, u32[]{:S(2)}) %collective-permute-start) | collective-permute-done | bytes 589856 | tf_op jit(solution)/shard_map/ppermute | solution.py:190
  11.8 2.1 %collective-permute-start.1 = (bf16[192,1536]{1,0:T(8,128)(2,1)S(1)}, bf16[192,1536]{1,0:T(8,128)(2,1)S(1)}, u32[]{:S(2)}, u32[]{:S(2)}) collective-permute-start(bf16[192,1536]{1,0:T(8,128)(2,1)S(1)} %collective-permute-done.rest_1_), channel_id=1, source_target_pairs={{0,2},{2,4},{4,6},{6,7},{7,5},{5,3},{3,1},{1,0},{8,9},{10,8},{12,1... | collective-permute-start | bytes 1769480 | tf_op jit(solution)/shard_map/ppermute | solution.py:190
  13.8 7.8 %collective-permute-done.1.rest_2_ = bf16[192,1536]{1,0:T(8,128)(2,1)S(1)} collective-permute-done((bf16[192,1536]{1,0:T(8,128)(2,1)S(1)}, bf16[192,1536]{1,0:T(8,128)(2,1)S(1)}, u32[]{:S(2)}, u32[]{:S(2)}) %collective-permute-start.1) | collective-permute-done | bytes 589856 | tf_op jit(solution)/shard_map/ppermute | solution.py:190
  21.6 2.1 %collective-permute-start.2 = (bf16[192,1536]{1,0:T(8,128)(2,1)S(1)}, bf16[192,1536]{1,0:T(8,128)(2,1)}, u32[]{:S(2)}, u32[]{:S(2)}) collective-permute-start(bf16[192,1536]{1,0:T(8,128)(2,1)S(1)} %collective-permute-done.1.rest_2_), channel_id=1, source_target_pairs={{0,2},{2,4},{4,6},{6,7},{7,5},{5,3},{3,1},{1,0},{8,9},{10,8},{12,1... | collective-permute-start | bytes 1769480 | tf_op jit(solution)/shard_map/ppermute | solution.py:190
  23.7 0.5 collective-permute-start.4
  24.2 7.4 %collective-permute-done.2.rest_3_ = bf16[192,1536]{1,0:T(8,128)(2,1)} collective-permute-done((bf16[192,1536]{1,0:T(8,128)(2,1)S(1)}, bf16[192,1536]{1,0:T(8,128)(2,1)}, u32[]{:S(2)}, u32[]{:S(2)}) %collective-permute-start.2) | collective-permute-done | bytes 589856 | tf_op jit(solution)/shard_map/ppermute | solution.py:190
  31.6 2.1 %collective-permute-start.6 = (bf16[192,1536]{1,0:T(8,128)(2,1)}, bf16[192,1536]{1,0:T(8,128)(2,1)}, u32[]{:S(2)}, u32[]{:S(2)}) collective-permute-start(bf16[192,1536]{1,0:T(8,128)(2,1)} %collective-permute-done.2.rest_3_), channel_id=1, source_target_pairs={{0,2},{2,4},{4,6},{6,7},{7,5},{5,3},{3,1},{1,0},{8,9},{10,8},{12,1... | collective-permute-start | bytes 1769480 | tf_op jit(solution)/shard_map/ppermute | solution.py:190
  33.7 0.5 collective-permute-start.7
  34.2 1.3 reshape.25.gain_ref
  35.5 0.7 pad_add_fusion.meta
  36.2 5.7 %collective-permute-done.6.rest_7_ = bf16[192,1536]{1,0:T(8,128)(2,1)} collective-permute-done((bf16[192,1536]{1,0:T(8,128)(2,1)}, bf16[192,1536]{1,0:T(8,128)(2,1)}, u32[]{:S(2)}, u32[]{:S(2)}) %collective-permute-start.6) | collective-permute-done | bytes 589856 | tf_op jit(solution)/shard_map/ppermute | solution.py:190
  41.8 11.0 %forward_rows.1 = (bf16[2,320,1536]{2,1,0:T(8,128)(2,1)}, f32[32,8,128]{2,1,0:T(8,128)}) custom-call(s32[2]{0:T(128)} %pad_add_fusion.meta, s32[128]{0:T(128)} %constant.31.clone.table, s32[64]{0:T(128)} %lens.1, f32[64]{0:T(128)} %offs.1, bf16[2,320,1536]{2,1,0:T(8,128)(2,1)} %o_ref.1, bf16[2,320,1536]{2,1,0:T(8,128)(2,1)} %x_ref.1, ...), custom_call_target="tpu_custom_call" | custom-call | flops 3019898880 | bytes 12582912 | tf_op jit(solution)/shard_map/forward_rows/pallas_call | solution.py:216
  52.8 0.1 collective-permute-start.8
  52.9 6.4 %all-to-all-start = ((f32[32,8,128]{2,1,0:T(8,128)}), f32[32,8,128]{2,1,0:T(8,128)S(1)}, u32[]{:S(2)}, u32[]{:S(2)}) async-start(f32[32,8,128]{2,1,0:T(8,128)} %get-tuple-element.10), calls=%async_computation | async-start | bytes 262144 | tf_op jit(solution)/shard_map/all_to_all | solution.py:245
  59.4 2.5 %copy.27 = bf16[2,320,1536]{1,2,0:T(8,128)(2,1)} copy(bf16[2,320,1536]{2,1,0:T(8,128)(2,1)S(1)} %copy-done.1) | data formatting | bytes 3932160 | tf_op args[1]
  61.8 0.1 reshape.26
  61.9 0.6 pad.4.pidm
  62.6 4.1 %copy.29.ot_par = bf16[2,1536,320]{2,1,0:T(8,128)(2,1)} copy(bf16[2,1536,320]{1,2,0:T(8,128)(2,1)} %collective-permute-done.7) | data formatting | bytes 3932160 | tf_op jit(solution)/shard_map/ppermute | solution.py:193
  66.6 0.5 all-to-all-done.recv
  67.2 0.7 copy-done.2
  67.8 4.0 %first_rows.1 = (bf16[192,768]{1,0:T(8,128)(2,1)}, f32[8,128]{1,0:T(8,128)}) custom-call(s32[2]{0:T(128)} %pad_add_fusion.meta, s32[128]{0:T(128)} %constant.31.clone.table, s32[64]{0:T(128)} %pids.1, f32[32,8,128]{2,1,0:T(8,128)} %copy-done.2, s32[32,128]{1,0:T(8,128)} %pad.4.pidm, bf16[2,1536,320]{2,1,0:T(8,128)(2,1)} %bitcast.18, ...), custom_call_target="tpu_custom_call" | custom-call | flops 377487360 | bytes 2457600 | tf_op jit(solution)/shard_map/first_rows/pallas_call | solution.py:256
  71.8 1.3 collective-permute-start.9
  73.1 10.6 %rest_rows.1 = bf16[7,192,768]{2,1,0:T(8,128)(2,1)} custom-call(s32[2]{0:T(128)} %pad_add_fusion.meta, s32[128]{0:T(128)} %constant.31.clone.table, f32[8,128]{1,0:T(8,128)} %get-tuple-element.12.c_ref, bf16[2,1536,320]{2,1,0:T(8,128)(2,1)} %bitcast.19, bf16[2,1536,320]{2,1,0:T(8,128)(2,1)} %copy.29.ot_par, ...), custom_call_target="tpu_custom_call" | custom-call | flops 3019898880 | bytes 10223616 | tf_op jit(solution)/shard_map/rest_rows/pallas_call | solution.py:288
  83.6 1.1 slice.38
  84.8 1.0 fusion.2
  85.9 1.5 %collective-permute-start.10 = (bf16[2,192,768]{2,1,0:T(8,128)(2,1)S(1)}, bf16[2,192,768]{2,1,0:T(8,128)(2,1)S(1)}, u32[]{:S(2)}, u32[]{:S(2)}) collective-permute-start(bf16[2,192,768]{2,1,0:T(8,128)(2,1)S(1)} %pad_maximum_fusion.1), channel_id=1, source_target_pairs={{0,2},{2,4},{4,6},{6,7},{7,5},{5,3},{3,1},{1,0},{8,9},{10,8},{12,1... | collective-permute-start | bytes 1769480 | tf_op jit(solution)/shard_map/ppermute | solution.py:190
  87.4 8.4 %collective-permute-done.10 = bf16[2,192,768]{2,1,0:T(8,128)(2,1)S(1)} collective-permute-done((bf16[2,192,768]{2,1,0:T(8,128)(2,1)S(1)}, bf16[2,192,768]{2,1,0:T(8,128)(2,1)S(1)}, u32[]{:S(2)}, u32[]{:S(2)}) %collective-permute-start.10) | collective-permute-done | bytes 589856 | tf_op jit(solution)/shard_map/ppermute | solution.py:190
  95.8 0.1 add_convert_fusion.1
  96.0 1.5 %collective-permute-start.11 = (bf16[2,192,768]{2,1,0:T(8,128)(2,1)S(1)}, bf16[2,192,768]{2,1,0:T(8,128)(2,1)S(1)}, u32[]{:S(2)}, u32[]{:S(2)}) collective-permute-start(bf16[2,192,768]{2,1,0:T(8,128)(2,1)S(1)} %add_convert_fusion.1), channel_id=1, source_target_pairs={{0,2},{2,4},{4,6},{6,7},{7,5},{5,3},{3,1},{1,0},{8,9},{10,8},{12,1... | collective-permute-start | bytes 1769480 | tf_op jit(solution)/shard_map/ppermute | solution.py:190
  97.5 8.4 %collective-permute-done.11 = bf16[2,192,768]{2,1,0:T(8,128)(2,1)S(1)} collective-permute-done((bf16[2,192,768]{2,1,0:T(8,128)(2,1)S(1)}, bf16[2,192,768]{2,1,0:T(8,128)(2,1)S(1)}, u32[]{:S(2)}, u32[]{:S(2)}) %collective-permute-start.11) | collective-permute-done | bytes 589856 | tf_op jit(solution)/shard_map/ppermute | solution.py:190
  105.9 0.1 add_convert_fusion
  106.0 1.5 %collective-permute-start.12 = (bf16[2,192,768]{2,1,0:T(8,128)(2,1)S(1)}, bf16[2,192,768]{2,1,0:T(8,128)(2,1)S(1)}, u32[]{:S(2)}, u32[]{:S(2)}) collective-permute-start(bf16[2,192,768]{2,1,0:T(8,128)(2,1)S(1)} %add_convert_fusion), channel_id=1, source_target_pairs={{0,2},{2,4},{4,6},{6,7},{7,5},{5,3},{3,1},{1,0},{8,9},{10,8},{12,1... | collective-permute-start | bytes 1769480 | tf_op jit(solution)/shard_map/ppermute | solution.py:190
  107.6 8.4 %collective-permute-done.12 = bf16[2,192,768]{2,1,0:T(8,128)(2,1)S(1)} collective-permute-done((bf16[2,192,768]{2,1,0:T(8,128)(2,1)S(1)}, bf16[2,192,768]{2,1,0:T(8,128)(2,1)S(1)}, u32[]{:S(2)}, u32[]{:S(2)}) %collective-permute-start.12) | collective-permute-done | bytes 589856 | tf_op jit(solution)/shard_map/ppermute | solution.py:190
  116.1 1.6 %collective-permute-done.13 = bf16[192,768]{1,0:T(8,128)(2,1)S(1)} collective-permute-done((bf16[192,768]{1,0:T(8,128)(2,1)S(1)}, bf16[192,768]{1,0:T(8,128)(2,1)S(1)}, u32[]{:S(2)}, u32[]{:S(2)}) %collective-permute-start.13) | collective-permute-done | bytes 294944 | tf_op jit(solution)/shard_map/ppermute | solution.py:193
  117.6 0.1 fusion.1
  117.8 1.5 %collective-permute-start.14 = (bf16[192,768]{1,0:T(8,128)(2,1)S(1)}, bf16[192,768]{1,0:T(8,128)(2,1)S(1)}, u32[]{:S(2)}, u32[]{:S(2)}) collective-permute-start(bf16[192,768]{1,0:T(8,128)(2,1)S(1)} %fusion.1), channel_id=1, source_target_pairs={{0,16},{8,24},{16,0},{24,8},{1,17},{9,25},{17,1},{25,9},{2,18},{10... | collective-permute-start | bytes 884744 | tf_op jit(solution)/shard_map/ppermute | solution.py:342
  119.3 0.9 slice_reduce_fusion
  120.2 0.1 mul.22
  120.3 0.1 select_reduce_fusion.1
  120.5 6.4 %collective-permute-done.14 = bf16[192,768]{1,0:T(8,128)(2,1)S(1)} collective-permute-done((bf16[192,768]{1,0:T(8,128)(2,1)S(1)}, bf16[192,768]{1,0:T(8,128)(2,1)S(1)}, u32[]{:S(2)}, u32[]{:S(2)}) %collective-permute-start.14) | collective-permute-done | bytes 294944 | tf_op jit(solution)/shard_map/ppermute | solution.py:342
  126.9 0.1 add_multiply_fusion
  127.0 0.1 select_reduce_fusion
  127.1 0.1 reduce_sum.31
  127.2 1.6 %multiply_reduce_fusion = f32[]{:T(128)} fusion(f32[32,1,2]{2,1,0:T(1,128)S(1)} %bitcast.21, f32[32,8,128]{2,1,0:T(8,128)} %copy-done.2), kind=kLoop, calls=%fused_computation.14 | loop fusion | flops 191 | bytes 516 | tf_op jit(solution)/shard_map/reduce_sum | solution.py:357
  129.4 12.2 %attn_rows.1 = (bf16[2,320,1536]{2,1,0:T(8,128)(2,1)}, bf16[2,320,1536]{2,1,0:T(8,128)(2,1)}) custom-call(s32[2]{0:T(128)} %pad_add_fusion.meta, s32[128]{0:T(128)} %constant.31.clone.table, f32[8,128]{1,0:T(8,128)} %get-tuple-element.12.c_ref, bf16[2,320,1536]{2,1,0:T(8,128)(2,1)} %get-tuple-element.11.r_own.r_ref, bf16[192,1536]{1,0:T(8,128)(2,1)} %rest_0_.3, ...), custom_call_target="tpu_custom_call" | custom-call | flops 3019898880 | bytes 10616832 | tf_op jit(solution)/shard_map/attn_rows/pallas_call | solution.py:311
  141.6 0.1 broadcast_select_fusion.1
  141.7 1.2 pad_maximum_fusion
  (27 shorter events, 0.3 us)
Async XLA Ops:
  0.6 11.1 %collective-permute-start = (bf16[192,1536]{1,0:T(8,128)(2,1)}, bf16[192,1536]{1,0:T(8,128)(2,1)S(1)}, u32[]{:S(2)}, u32[]{:S(2)}) collective-permute-start(bf16[192,1536]{1,0:T(8,128)(2,1)} %rest_0_.3), channel_id=1, source_target_pairs={{0,2},{2,4},{4,6},{6,7},{7,5},{5,3},{3,1},{1,0},{8,9},{10,8},{12,1... | collective-permute-start | bytes 1769480 | tf_op jit(solution)/shard_map/ppermute | solution.py:190
  11.8 30.1 %copy-start.5 = (bf16[192,1536]{1,0:T(8,128)(2,1)}, bf16[192,1536]{1,0:T(8,128)(2,1)S(1)}, u32[]{:S(2)}) copy-start(bf16[192,1536]{1,0:T(8,128)(2,1)S(1)} %collective-permute-done.rest_1_) | copy-start | bytes 1769476
  11.8 9.9 %collective-permute-start.1 = (bf16[192,1536]{1,0:T(8,128)(2,1)S(1)}, bf16[192,1536]{1,0:T(8,128)(2,1)S(1)}, u32[]{:S(2)}, u32[]{:S(2)}) collective-permute-start(bf16[192,1536]{1,0:T(8,128)(2,1)S(1)} %collective-permute-done.rest_1_), channel_id=1, source_target_pairs={{0,2},{2,4},{4,6},{6,7},{7,5},{5,3},{3,1},{1,0},{8,9},{10,8},{12,1... | collective-permute-start | bytes 1769480 | tf_op jit(solution)/shard_map/ppermute | solution.py:190
  21.6 20.2 %copy-start.6 = (bf16[192,1536]{1,0:T(8,128)(2,1)}, bf16[192,1536]{1,0:T(8,128)(2,1)S(1)}, u32[]{:S(2)}) copy-start(bf16[192,1536]{1,0:T(8,128)(2,1)S(1)} %collective-permute-done.1.rest_2_) | copy-start | bytes 1769476
  21.6 10.0 %collective-permute-start.2 = (bf16[192,1536]{1,0:T(8,128)(2,1)S(1)}, bf16[192,1536]{1,0:T(8,128)(2,1)}, u32[]{:S(2)}, u32[]{:S(2)}) collective-permute-start(bf16[192,1536]{1,0:T(8,128)(2,1)S(1)} %collective-permute-done.1.rest_2_), channel_id=1, source_target_pairs={{0,2},{2,4},{4,6},{6,7},{7,5},{5,3},{3,1},{1,0},{8,9},{10,8},{12,1... | collective-permute-start | bytes 1769480 | tf_op jit(solution)/shard_map/ppermute | solution.py:190
  23.7 12.5 %collective-permute-start.3 = (bf16[192,1536]{1,0:T(8,128)(2,1)S(1)}, bf16[192,1536]{1,0:T(8,128)(2,1)}, u32[]{:S(2)}, u32[]{:S(2)}) collective-permute-start(bf16[192,1536]{1,0:T(8,128)(2,1)S(1)} %collective-permute-done.rest_1_), channel_id=1, source_target_pairs={{0,8},{8,0},{16,24},{24,16},{1,9},{9,1},{17,25},{25,17},{2,10},{10... | collective-permute-start | bytes 1769480 | tf_op jit(solution)/shard_map/ppermute | solution.py:193
  23.7 12.5 %collective-permute-start.4 = (bf16[192,1536]{1,0:T(8,128)(2,1)S(1)}, bf16[192,1536]{1,0:T(8,128)(2,1)}, u32[]{:S(2)}, u32[]{:S(2)}) collective-permute-start(bf16[192,1536]{1,0:T(8,128)(2,1)S(1)} %collective-permute-done.1.rest_2_), channel_id=1, source_target_pairs={{0,8},{8,0},{16,24},{24,16},{1,9},{9,1},{17,25},{25,17},{2,10},{10... | collective-permute-start | bytes 1769480 | tf_op jit(solution)/shard_map/ppermute | solution.py:193
  31.6 10.2 %collective-permute-start.6 = (bf16[192,1536]{1,0:T(8,128)(2,1)}, bf16[192,1536]{1,0:T(8,128)(2,1)}, u32[]{:S(2)}, u32[]{:S(2)}) collective-permute-start(bf16[192,1536]{1,0:T(8,128)(2,1)} %collective-permute-done.2.rest_3_), channel_id=1, source_target_pairs={{0,2},{2,4},{4,6},{6,7},{7,5},{5,3},{3,1},{1,0},{8,9},{10,8},{12,1... | collective-permute-start | bytes 1769480 | tf_op jit(solution)/shard_map/ppermute | solution.py:190
  33.7 8.1 %collective-permute-start.5 = (bf16[192,1536]{1,0:T(8,128)(2,1)}, bf16[192,1536]{1,0:T(8,128)(2,1)}, u32[]{:S(2)}, u32[]{:S(2)}) collective-permute-start(bf16[192,1536]{1,0:T(8,128)(2,1)} %collective-permute-done.2.rest_3_), channel_id=1, source_target_pairs={{0,8},{8,0},{16,24},{24,16},{1,9},{9,1},{17,25},{25,17},{2,10},{10... | collective-permute-start | bytes 1769480 | tf_op jit(solution)/shard_map/ppermute | solution.py:193
  33.7 28.8 %collective-permute-start.7 = (bf16[2,1536,320]{1,2,0:T(8,128)(2,1)}, bf16[2,1536,320]{1,2,0:T(8,128)(2,1)}, u32[]{:S(2)}, u32[]{:S(2)}) collective-permute-start(bf16[2,1536,320]{1,2,0:T(8,128)(2,1)} %bitcast.20), channel_id=1, source_target_pairs={{0,8},{8,0},{16,24},{24,16},{1,9},{9,1},{17,25},{25,17},{2,10},{10... | collective-permute-start | bytes 5898248 | tf_op jit(solution)/shard_map/ppermute | solution.py:193
  36.2 23.2 %copy-start.1 = (bf16[2,320,1536]{2,1,0:T(8,128)(2,1)S(1)}, bf16[2,320,1536]{2,1,0:T(8,128)(2,1)}, u32[]{:S(2)}) copy-start(bf16[2,320,1536]{2,1,0:T(8,128)(2,1)} %o_ref.1) | copy-start | bytes 5898244
  52.8 14.3 %collective-permute-start.8 = (bf16[2,320,1536]{2,1,0:T(8,128)(2,1)}, bf16[2,320,1536]{2,1,0:T(8,128)(2,1)}, u32[]{:S(2)}, u32[]{:S(2)}) collective-permute-start(bf16[2,320,1536]{2,1,0:T(8,128)(2,1)} %get-tuple-element.11.r_own.r_ref), channel_id=1, source_target_pairs={{0,8},{8,0},{16,24},{24,16},{1,9},{9,1},{17,25},{25,17},{2,10},{10... | collective-permute-start | bytes 5898248 | tf_op jit(solution)/shard_map/ppermute | solution.py:193
  52.9 14.3 %all-to-all-start = ((f32[32,8,128]{2,1,0:T(8,128)}), f32[32,8,128]{2,1,0:T(8,128)S(1)}, u32[]{:S(2)}, u32[]{:S(2)}) async-start(f32[32,8,128]{2,1,0:T(8,128)} %get-tuple-element.10), calls=%async_computation | async-start | bytes 262144 | tf_op jit(solution)/shard_map/all_to_all | solution.py:245
  59.4 2.5 %copy-start.3 = (s32[64]{0:T(128)S(1)}, s32[64]{0:T(128)}, u32[]{:S(2)}) copy-start(s32[64]{0:T(128)} %pids.1) | copy-start | bytes 772
  67.1 0.7 copy-start.2
  71.8 13.0 %collective-permute-start.9 = (bf16[192,768]{1,0:T(8,128)(2,1)}, bf16[192,768]{1,0:T(8,128)(2,1)S(1)}, u32[]{:S(2)}, u32[]{:S(2)}) collective-permute-start(bf16[192,768]{1,0:T(8,128)(2,1)} %get-tuple-element.15), channel_id=1, source_target_pairs={{0,2},{2,4},{4,6},{6,7},{7,5},{5,3},{3,1},{1,0},{8,9},{10,8},{12,1... | collective-permute-start | bytes 884744 | tf_op jit(solution)/shard_map/ppermute | solution.py:190
  83.6 12.2 %copy-start = (bf16[7,192,768]{2,1,0:T(8,128)(2,1)S(1)}, bf16[7,192,768]{2,1,0:T(8,128)(2,1)}, u32[]{:S(2)}) copy-start(bf16[7,192,768]{2,1,0:T(8,128)(2,1)} %rest_rows.1) | copy-start | bytes 6193156
  85.9 9.9 %collective-permute-start.10 = (bf16[2,192,768]{2,1,0:T(8,128)(2,1)S(1)}, bf16[2,192,768]{2,1,0:T(8,128)(2,1)S(1)}, u32[]{:S(2)}, u32[]{:S(2)}) collective-permute-start(bf16[2,192,768]{2,1,0:T(8,128)(2,1)S(1)} %pad_maximum_fusion.1), channel_id=1, source_target_pairs={{0,2},{2,4},{4,6},{6,7},{7,5},{5,3},{3,1},{1,0},{8,9},{10,8},{12,1... | collective-permute-start | bytes 1769480 | tf_op jit(solution)/shard_map/ppermute | solution.py:190
  95.9 24.4 %copy-start.4 = (s32[64]{0:T(128)S(1)}, s32[64]{0:T(128)}, u32[]{:S(2)}) copy-start(s32[64]{0:T(128)} %pids.1) | copy-start | bytes 772
  96.0 9.9 %collective-permute-start.11 = (bf16[2,192,768]{2,1,0:T(8,128)(2,1)S(1)}, bf16[2,192,768]{2,1,0:T(8,128)(2,1)S(1)}, u32[]{:S(2)}, u32[]{:S(2)}) collective-permute-start(bf16[2,192,768]{2,1,0:T(8,128)(2,1)S(1)} %add_convert_fusion.1), channel_id=1, source_target_pairs={{0,2},{2,4},{4,6},{6,7},{7,5},{5,3},{3,1},{1,0},{8,9},{10,8},{12,1... | collective-permute-start | bytes 1769480 | tf_op jit(solution)/shard_map/ppermute | solution.py:190
  106.0 9.9 %collective-permute-start.12 = (bf16[2,192,768]{2,1,0:T(8,128)(2,1)S(1)}, bf16[2,192,768]{2,1,0:T(8,128)(2,1)S(1)}, u32[]{:S(2)}, u32[]{:S(2)}) collective-permute-start(bf16[2,192,768]{2,1,0:T(8,128)(2,1)S(1)} %add_convert_fusion), channel_id=1, source_target_pairs={{0,2},{2,4},{4,6},{6,7},{7,5},{5,3},{3,1},{1,0},{8,9},{10,8},{12,1... | collective-permute-start | bytes 1769480 | tf_op jit(solution)/shard_map/ppermute | solution.py:190
  116.0 1.6 %collective-permute-start.13 = (bf16[192,768]{1,0:T(8,128)(2,1)S(1)}, bf16[192,768]{1,0:T(8,128)(2,1)S(1)}, u32[]{:S(2)}, u32[]{:S(2)}) collective-permute-start(bf16[192,768]{1,0:T(8,128)(2,1)S(1)} %slice_bitcast_fusion), channel_id=1, source_target_pairs={{0,8},{8,0},{16,24},{24,16},{1,9},{9,1},{17,25},{25,17},{2,10},{10... | collective-permute-start | bytes 884744 | tf_op jit(solution)/shard_map/ppermute | solution.py:193
  117.8 9.1 %collective-permute-start.14 = (bf16[192,768]{1,0:T(8,128)(2,1)S(1)}, bf16[192,768]{1,0:T(8,128)(2,1)S(1)}, u32[]{:S(2)}, u32[]{:S(2)}) collective-permute-start(bf16[192,768]{1,0:T(8,128)(2,1)S(1)} %fusion.1), channel_id=1, source_target_pairs={{0,16},{8,24},{16,0},{24,8},{1,17},{9,25},{17,1},{25,9},{2,18},{10... | collective-permute-start | bytes 884744 | tf_op jit(solution)/shard_map/ppermute | solution.py:342
  127.0 14.7 %collective-permute-start.15 = (f32[192,768]{1,0:T(8,128)S(1)}, f32[192,768]{1,0:T(8,128)S(1)}, u32[]{:S(2)}, u32[]{:S(2)}) collective-permute-start(f32[192,768]{1,0:T(8,128)S(1)} %add_multiply_fusion), channel_id=1, source_target_pairs={{0,8},{8,0},{16,24},{24,16},{1,9},{9,1},{17,25},{25,17},{2,10},{10... | collective-permute-start | bytes 1769480 | tf_op jit(solution)/shard_map/ppermute | solution.py:193
